TPU v7x, 256 devices: a whole 4x4x8 slice. The times are simulated.
256 devices in a mesh: ctx: 64 (over z, x, core), dp: 4 (over y).
Axes of the slice: x: 4, y: 4, z: 8, core: 2. Of those that a mesh axis runs over, the one named last changes fastest.
Arguments:
- query_policy: bfloat16 [4, 2, 8192, 2048], P('dp', None, 'ctx'), may hold values from -6 to 6
- key_policy: bfloat16 [4, 2, 8192, 512], P('dp', None, 'ctx'), may hold values from -6 to 6
- value_policy: bfloat16 [4, 2, 8192, 512], P('dp', None, 'ctx'), may hold values from -60 to 60
- query_reference: bfloat16 [4, 2, 8192, 2048], P('dp', None, 'ctx'), may hold values from -6 to 6
- key_reference: bfloat16 [4, 2, 8192, 512], P('dp', None, 'ctx'), may hold values from -6 to 6
- value_reference: bfloat16 [4, 2, 8192, 512], P('dp', None, 'ctx'), may hold values from -60 to 60
- readout: bfloat16 [4, 2, 8192, 2048], P('dp', None, 'ctx'), may hold values from -0.0029296875 to 0.0029296875
- response_mask: int32 [4, 2, 8192], P('dp', None, 'ctx'), may hold values from 0 to 1, as said below
Outputs:
- query_gradient_rows: bfloat16 [4, 2, 8192, 2048], P('dp', None, 'ctx')
- key_gradient_rows: bfloat16 [4, 2, 8192, 512], P('dp', None, 'ctx')
- value_gradient_rows: bfloat16 [4, 2, 8192, 512], P('dp', None, 'ctx')
- pair_loss: float32 [], replicated
Inputs may be any that keep to these rules, and one draw needn't show every extreme that they name: `response_mask`: in each pair the mask is 1 exactly from the prompt's end (1 to 2048, the same for both sequences) up to but excluding the sequence's own end (4096 to 8192).
All inputs are finite; a program needn't handle non-finite values.
Results may differ from a plain program's by a relative error of at most 0.018.
Values may be sent and summed in bfloat16 or wider, within the bound.
No kernel may reach another device: no remote copies, remote signals or barrier semaphores. Data moves between devices by JAX's collectives and lax.ppermute only.
A program may use at most 192 MiB of HBM per device.

v0:
```python
import math
import jax
import jax.numpy as jnp
from jax import lax
from jax.sharding import PartitionSpec as P

HEADS = 16
KV_HEADS = 4
D_HEAD = 128
dpo_beta = 0.5
epsilon = 1e-06


def carried_in(x, axis, join, neutral, backward):
    count = lax.axis_size(axis)
    place = lax.axis_index(axis)
    ahead = count - 1 - place if backward else place
    gathered = lax.all_gather(x.astype(jnp.bfloat16), axis)
    state = jnp.zeros_like(x) + jnp.asarray(neutral, x.dtype)

    def one(turn, state):
        source = count - 1 - turn if backward else turn
        return join(state, lax.dynamic_index_in_dim(gathered, source, 0, False).astype(x.dtype))

    return lax.fori_loop(0, ahead, one, state)


def add_states(earlier, following):
    return earlier + following


def causal_mask(block_rows):
    positions = jnp.arange(block_rows)
    return positions[:, None] >= positions[None, :]


def span_state(key_head_rows, value_head_rows):
    return jnp.einsum(
        "asgd,asge->agde", key_head_rows, value_head_rows, preferred_element_type=jnp.float32
    )


def span_forward(query_head_rows, key_head_rows, value_head_rows, carried):
    causal = causal_mask(query_head_rows.shape[1])
    pair_score_rows = jnp.einsum(
        "atgrd,asgd->agrts", query_head_rows, key_head_rows, preferred_element_type=jnp.float32
    )
    pair_score_rows = jnp.where(causal, pair_score_rows, 0.0).astype(jnp.bfloat16)
    carried_low = carried.astype(jnp.bfloat16)
    unnormed_output = jnp.einsum(
        "agrts,asgd->atgrd", pair_score_rows, value_head_rows, preferred_element_type=jnp.float32
    )
    unnormed_output = unnormed_output + jnp.einsum(
        "atgrd,agde->atgre", query_head_rows, carried_low, preferred_element_type=jnp.float32
    )
    inverse = lax.rsqrt(
        jnp.mean(unnormed_output * unnormed_output, axis=-1, keepdims=True) + epsilon
    )
    return (pair_score_rows, carried_low, unnormed_output * inverse, inverse)


def shards(
    query_policy,
    key_policy,
    value_policy,
    query_reference,
    key_reference,
    value_reference,
    readout,
    response_mask,
):
    block_rows = query_policy.shape[2]
    per_group = HEADS // KV_HEADS

    def split_query(array):
        return array.reshape(2, block_rows, KV_HEADS, per_group, D_HEAD)

    def split_shared(array):
        return array.reshape(2, block_rows, KV_HEADS, D_HEAD)

    query_pol = split_query(query_policy)
    key_pol = split_shared(key_policy)
    value_pol = split_shared(value_policy)
    query_ref = split_query(query_reference)
    key_ref = split_shared(key_reference)
    value_ref = split_shared(value_reference)
    states_policy = span_state(key_pol, value_pol)
    states_reference = span_state(key_ref, value_ref)
    carried_policy = carried_in(
        states_policy, "ctx", add_states, jnp.zeros_like(states_policy), False
    )
    carried_reference = carried_in(
        states_reference, "ctx", add_states, jnp.zeros_like(states_reference), False
    )
    scores_policy, carried_policy_low, normed_policy, inverse_policy = span_forward(
        query_pol, key_pol, value_pol, carried_policy
    )
    normed_reference = span_forward(query_ref, key_ref, value_ref, carried_reference)[2]
    read_heads = split_query(readout)
    mask_rows = response_mask.reshape(2, block_rows).astype(jnp.float32)
    policy_tokens = jnp.sum(normed_policy * read_heads, axis=(2, 3, 4))
    reference_tokens = jnp.sum(normed_reference * read_heads, axis=(2, 3, 4))
    sums = jnp.stack(
        [jnp.sum(mask_rows * policy_tokens, axis=1), jnp.sum(mask_rows * reference_tokens, axis=1)]
    )
    totals = lax.psum(sums, "ctx")
    delta = totals[0, 0] - totals[0, 1] - (totals[1, 0] - totals[1, 1])
    pair_loss = lax.psum(jax.nn.softplus(-dpo_beta * delta), "dp") / lax.axis_size("dp")
    scale = math.sqrt(HEADS * D_HEAD * block_rows * lax.axis_size("ctx"))
    pull = dpo_beta * jax.nn.sigmoid(-dpo_beta * delta) * scale
    weights = jnp.stack([-pull, pull])
    upstream = (weights[:, None] * mask_rows)[:, :, None, None, None] * read_heads
    pulled_back_state = upstream - normed_policy * jnp.mean(
        upstream * normed_policy, axis=-1, keepdims=True
    )
    pulled_back_state = (pulled_back_state * inverse_policy).astype(jnp.bfloat16)
    block_grad = jnp.einsum(
        "atgrd,atgre->agde", query_pol, pulled_back_state, preferred_element_type=jnp.float32
    )
    later = carried_in(block_grad, "ctx", add_states, jnp.zeros_like(block_grad), True)
    later_low = later.astype(jnp.bfloat16)
    causal = causal_mask(block_rows)
    score_gradient = jnp.einsum(
        "atgre,asge->agrts", pulled_back_state, value_pol, preferred_element_type=jnp.float32
    )
    score_gradient = jnp.where(causal, score_gradient, 0.0).astype(jnp.bfloat16)
    query_gradient_rows = jnp.einsum(
        "agrts,asgd->atgrd", score_gradient, key_pol, preferred_element_type=jnp.float32
    )
    query_gradient_rows = query_gradient_rows + jnp.einsum(
        "atgre,agde->atgrd",
        pulled_back_state,
        carried_policy_low,
        preferred_element_type=jnp.float32,
    )
    key_gradient_rows = jnp.einsum(
        "agrts,atgrd->asgd", score_gradient, query_pol, preferred_element_type=jnp.float32
    )
    key_gradient_rows = key_gradient_rows + jnp.einsum(
        "asge,agde->asgd", value_pol, later_low, preferred_element_type=jnp.float32
    )
    value_gradient_rows = jnp.einsum(
        "agrts,atgre->asge", scores_policy, pulled_back_state, preferred_element_type=jnp.float32
    )
    value_gradient_rows = value_gradient_rows + jnp.einsum(
        "asgd,agde->asge", key_pol, later_low, preferred_element_type=jnp.float32
    )
    return (
        query_gradient_rows.reshape(1, 2, block_rows, HEADS * D_HEAD).astype(jnp.bfloat16),
        key_gradient_rows.reshape(1, 2, block_rows, KV_HEADS * D_HEAD).astype(jnp.bfloat16),
        value_gradient_rows.reshape(1, 2, block_rows, KV_HEADS * D_HEAD).astype(jnp.bfloat16),
        pair_loss,
    )


def solution(mesh):
    placed = (
        P("dp", None, "ctx", None),
        P("dp", None, "ctx", None),
        P("dp", None, "ctx", None),
        P("dp", None, "ctx", None),
        P("dp", None, "ctx", None),
        P("dp", None, "ctx", None),
        P("dp", None, "ctx", None),
        P("dp", None, "ctx"),
    )
    return jax.shard_map(
        shards,
        mesh=mesh,
        in_specs=placed,
        out_specs=(
            P("dp", None, "ctx", None),
            P("dp", None, "ctx", None),
            P("dp", None, "ctx", None),
            P(),
        ),
        check_vma=False,
    )
```

profile of v0, /device:TPU:1, one launch (start us, length us, event | category | flops | bytes accessed | tf_op | source)
XLA Modules:
  0.0 600.7 jit_solution(8161237302858355317)
XLA Ops:
  8.3 1.1 reshape.127
  13.5 2.0 reshape.129
  15.5 3.0 copy.51
  18.5 1.5 fusion.2
  20.1 95.2 %all-gather.7.cloned.1.call-done = bf16[128,4,128,128]{3,2,1,0:T(8,128)(2,1)} async-done(((bf16[2,4,128,128]{3,2,1,0:T(8,128)(2,1)}), bf16[128,4,128,128]{3,2,1,0:T(8,128)(2,1)}) %all-gather.7.cloned.1.call-update) | async-done | bytes 16777232 | tf_op jit(solution)/shard_map/all_gather | solution.py:18
  115.3 1.1 while.32
  115.4 1.1 convert_add_fusion.6
  116.5 1.8 fusion.18
  118.3 97.1 %all-gather.9.cloned.1.call-done = bf16[128,4,128,128]{3,2,1,0:T(8,128)(2,1)} async-done(((bf16[2,4,128,128]{3,2,1,0:T(8,128)(2,1)}), bf16[128,4,128,128]{3,2,1,0:T(8,128)(2,1)}) %all-gather.9.cloned.1.call-update) | async-done | bytes 16777232 | tf_op jit(solution)/shard_map/all_gather | solution.py:18
  215.4 1.1 while.33
  216.6 1.8 fusion.13
  219.7 4.1 multiply_reduce_fusion.2
  223.8 2.8 multiply_reduce_fusion.3
  226.8 188.1 %psum.14 = f32[2,2]{1,0:T(2,128)S(1)} all-reduce(f32[2,2]{1,0:T(2,128)S(1)} %pad_maximum_fusion), channel_id=1, replica_groups=mesh['ctx'=64,'dp'=4] {'ctx'}, use_global_device_ids=true, to_apply=%region_10.11 | all-reduce | flops 4 | bytes 32 | tf_op jit(solution)/shard_map/psum | solution.py:106
  418.3 2.3 multiply_reduce_fusion
  423.8 9.0 %psum.15 = f32[]{:T(128)} all-reduce(f32[]{:T(128)S(6)} %select_n.32), channel_id=1, replica_groups=mesh['ctx'=64,'dp'=4] {'dp'}, use_global_device_ids=true, to_apply=%region_14.15 | all-reduce | flops 1 | bytes 8 | tf_op jit(solution)/shard_map/psum | solution.py:108
  432.7 1.7 fusion.3
  435.0 1.2 copy-done.6
  436.1 1.5 fusion
  437.6 2.4 copy.69
  440.6 2.6 convolution_bitcast_fusion.1
  443.7 78.9 %all-gather.11.cloned.1.call-done = bf16[128,4,128,128]{3,2,1,0:T(8,128)(2,1)} async-done(((bf16[2,4,128,128]{3,2,1,0:T(8,128)(2,1)}), bf16[128,4,128,128]{3,2,1,0:T(8,128)(2,1)}) %all-gather.11.cloned.1.call-update) | async-done | bytes 16777232 | tf_op jit(solution)/shard_map/all_gather | solution.py:18
  522.6 68.1 %while.34 = (s32[]{:T(128)}, f32[2,4,128,128]{3,2,1,0:T(8,128)S(1)}, s32[]{:T(128)}, bf16[64,2,4,128,128]{4,3,2,1,0:T(8,128)(2,1)}, s32[]{:T(128)}, /*index=5*/s32[]{:T(128)}, s32[]{:T(128)}, s32[]{:T(128)}) while((s32[]{:T(128)}, f32[2,4,128,128]{3,2,1,0:T(8,128)S(1)}, s32[]{:T(128)}, bf16[64,2,4,128,128]{4,3,2,1,0:T(8,128)(2,1)}, ...), condition=%wide.region_13.14_spmd, body=%wide.region_12.13_spmd.sunk | while | flops 262150 | bytes 1310855 | solution.py:25
  522.6 1.1 convert_add_fusion.8
  523.8 1.1 convert_add_fusion.8
  524.9 1.1 convert_add_fusion.8
  526.0 1.1 convert_add_fusion.8
  527.1 1.1 convert_add_fusion.8
  528.1 1.1 convert_add_fusion.8
  532.5 1.1 convert_add_fusion.8
  533.6 1.1 convert_add_fusion.8
  534.7 1.1 convert_add_fusion.8
  535.8 1.1 convert_add_fusion.8
  536.9 1.1 convert_add_fusion.8
  538.0 1.1 convert_add_fusion.8
  539.1 1.1 convert_add_fusion.8
  543.5 1.1 convert_add_fusion.8
  544.6 1.1 convert_add_fusion.8
  545.7 1.1 convert_add_fusion.8
  546.8 1.1 convert_add_fusion.8
  547.9 1.1 convert_add_fusion.8
  549.0 1.1 convert_add_fusion.8
  553.4 1.1 convert_add_fusion.8
  554.5 1.1 convert_add_fusion.8
  555.6 1.1 convert_add_fusion.8
  556.7 1.1 convert_add_fusion.8
  557.8 1.1 convert_add_fusion.8
  558.9 1.1 convert_add_fusion.8
  (109 shorter events, 54.4 us)
Async XLA Ops:
  7.2 3.3 copy-start.16
  7.2 3.4 copy-start.13
  7.2 108.1 %all-gather.7.cloned.1.call-start = ((), (), s32[]{:S(2)}) async-start(), calls=%async_computation | async-start | bytes 17039360 | tf_op jit(solution)/shard_map/all_gather | solution.py:18
  8.3 4.2 copy-start.12
  10.4 205.0 %all-gather.9.cloned.1.call-start = ((), (), s32[]{:S(2)}) async-start(), calls=%async_computation.1 | async-start | bytes 17039360 | tf_op jit(solution)/shard_map/all_gather | solution.py:18
  11.7 510.8 %all-gather.11.cloned.1.call-start = ((), (), s32[]{:S(2)}) async-start(), calls=%async_computation.2 | async-start | bytes 17039360 | tf_op jit(solution)/shard_map/all_gather | solution.py:18
  13.3 103.2 %copy-start.1 = (bf16[2,128,4,4,128]{4,3,2,1,0:T(4,128)(2,1)}, bf16[2,128,4,4,128]{4,3,2,1,0:T(4,128)(2,1)S(1)}, u32[]{:S(2)}) copy-start(bf16[2,128,4,4,128]{4,3,2,1,0:T(4,128)(2,1)S(1)} %reshape.126) | copy-start | bytes 3145732
  13.5 5.1 copy-start.14
  15.5 201.0 %copy-start.4 = (bf16[2,128,4,4,128]{4,3,2,1,0:T(4,128)(2,1)}, bf16[2,128,4,4,128]{4,3,2,1,0:T(4,128)(2,1)S(1)}, u32[]{:S(2)}) copy-start(bf16[2,128,4,4,128]{4,3,2,1,0:T(4,128)(2,1)S(1)} %reshape.129) | copy-start | bytes 3145732
  216.6 1.8 copy-start.7
  216.6 2.6 copy-start.10
  223.8 2.8 copy-start.17
  418.3 2.3 copy-start
  420.6 1.6 copy-start.2
  421.3 1.0 copy-start.5
  422.7 11.8 %copy-start.15 = (bf16[2,128,4,128,1]{1,3,4,2,0:T(8,128)(2,1)S(1)}, bf16[2,128,4,128,1]{1,3,4,2,0:T(8,128)(2,1)}, u32[]{:S(2)}) copy-start(bf16[2,128,4,128,1]{1,3,4,2,0:T(8,128)(2,1)} %copy-done.14) | copy-start | bytes 786436
  434.5 3.1 copy-start.8
  434.5 1.6 copy-start.6
  437.6 5.6 copy-start.3
  440.6 2.6 copy-start.9
  522.6 68.1 %copy-start.11 = (f32[2,4,128,128]{3,2,1,0:T(8,128)S(1)}, f32[2,4,128,128]{3,2,1,0:T(8,128)}, u32[]{:S(2)}) copy-start(f32[2,4,128,128]{3,2,1,0:T(8,128)} %convolution_bitcast_fusion.1) | copy-start | bytes 1572868
Sparse Core Ops, SparseCore 0:
  11.4 103.9 all-gather.6
  118.7 96.7 all-gather.8
  423.7 98.8 all-gather.10
where the time goes:
time: 605 us; the launch traced here: 601 us
  waiting for transfers between devices  271 us (45%)
  blocking collectives  197 us (33%)
  other arithmetic  74.6 us (12%)
  matrix products  19.5 us (3%)
  between operations  18.7 us (3%)
  local copies, waits for them, and re-layouts  17.8 us (3%)
    all_gather x3, waiting for transfers between devices, carried_in(): gathered = lax.all_gather(x.astype(jnp.bfloat16), axis)  271 us
    psum x1, blocking collectives, shards(): totals = lax.psum(sums, 'ctx')  188 us
    add x64, other arithmetic, add_states(): return earlier + following  68.5 us
  transfers between devices with their start and end apart: 3, of which 3 were waited for; matrix products, arithmetic and copies ran while one was open for 4% of the time, Pallas kernels for 0%

commit v1 on v0

--- a/solution.py
+++ b/solution.py
@@ -103,7 +103,7 @@
     sums = jnp.stack(
         [jnp.sum(mask_rows * policy_tokens, axis=1), jnp.sum(mask_rows * reference_tokens, axis=1)]
     )
-    totals = lax.psum(sums, "ctx")
+    totals = jnp.sum(lax.all_gather(sums, "ctx"), axis=0)
     delta = totals[0, 0] - totals[0, 1] - (totals[1, 0] - totals[1, 1])
     pair_loss = lax.psum(jax.nn.softplus(-dpo_beta * delta), "dp") / lax.axis_size("dp")
     scale = math.sqrt(HEADS * D_HEAD * block_rows * lax.axis_size("ctx"))

time: 605 us -> 522 us (0.86)
  blocking collectives: 197 us -> 117 us
    psum x1 -> x0, blocking collectives: 188 us -> none  [shards(): totals = lax.psum(sums, 'ctx')]
    all_gather x0 -> x1, blocking collectives: none -> 108 us  [shards(): totals = jnp.sum(lax.all_gather(sums, 'ctx'), axis=0)]
where the time goes in v1:
time: 522 us; the launch traced here: 517 us
  waiting for transfers between devices  268 us (51%)
  blocking collectives  117 us (22%)
  other arithmetic  74.6 us (14%)
  matrix products  19.5 us (4%)
  between operations  18.6 us (4%)
  local copies, waits for them, and re-layouts  17.8 us (3%)
    all_gather x3, waiting for transfers between devices, carried_in(): gathered = lax.all_gather(x.astype(jnp.bfloat16), axis)  268 us
    all_gather x1, blocking collectives, shards(): totals = jnp.sum(lax.all_gather(sums, 'ctx'), axis=0)  108 us
    add x64, other arithmetic, add_states(): return earlier + following  68.5 us
  transfers between devices with their start and end apart: 3, of which 3 were waited for; matrix products, arithmetic and copies ran while one was open for 4% of the time, Pallas kernels for 0%

profile of v1, /device:TPU:1, one launch (start us, length us, event | category | flops | bytes accessed | tf_op | source)
XLA Modules:
  0.0 517.1 jit_solution(17892208404402661106)
XLA Ops:
  8.3 1.1 reshape.127
  13.5 2.0 reshape.129
  15.5 3.0 copy.51
  18.5 1.5 fusion.2
  20.1 95.2 %all-gather.9.cloned.1.call-done = bf16[128,4,128,128]{3,2,1,0:T(8,128)(2,1)} async-done(((bf16[2,4,128,128]{3,2,1,0:T(8,128)(2,1)}), bf16[128,4,128,128]{3,2,1,0:T(8,128)(2,1)}) %all-gather.9.cloned.1.call-update) | async-done | bytes 16777232 | tf_op jit(solution)/shard_map/all_gather | solution.py:18
  115.3 1.1 while.32
  115.4 1.1 convert_add_fusion.6
  116.5 1.8 fusion.18
  118.3 97.1 %all-gather.11.cloned.1.call-done = bf16[128,4,128,128]{3,2,1,0:T(8,128)(2,1)} async-done(((bf16[2,4,128,128]{3,2,1,0:T(8,128)(2,1)}), bf16[128,4,128,128]{3,2,1,0:T(8,128)(2,1)}) %all-gather.11.cloned.1.call-update) | async-done | bytes 16777232 | tf_op jit(solution)/shard_map/all_gather | solution.py:18
  215.4 1.1 while.33
  216.6 1.8 fusion.13
  219.7 4.1 multiply_reduce_fusion.2
  223.8 2.8 multiply_reduce_fusion.3
  226.8 107.8 %all-gather.4 = f32[64,2,2]{2,1,0:T(2,128)S(1)} all-gather(f32[1,2,2]{2,1,0:T(2,128)S(1)} %maximum_bitcast_fusion), channel_id=4, replica_groups=mesh['ctx'=64,'dp'=4] {'ctx'}, dimensions={0}, use_global_device_ids=true | all-gather | bytes 1040 | tf_op jit(solution)/shard_map/all_gather | solution.py:106
  338.1 2.3 multiply_reduce_fusion
  343.5 9.0 %psum.7 = f32[]{:T(128)} all-reduce(f32[]{:T(128)S(6)} %select_n.32), channel_id=1, replica_groups=mesh['ctx'=64,'dp'=4] {'dp'}, use_global_device_ids=true, to_apply=%region_14.15 | all-reduce | flops 1 | bytes 8 | tf_op jit(solution)/shard_map/psum | solution.py:108
  352.5 1.7 fusion.3
  354.7 1.2 copy-done.6
  355.9 1.5 fusion
  357.3 2.4 copy.69
  360.4 2.6 convolution_bitcast_fusion.1
  363.4 75.6 %all-gather.13.cloned.1.call-done = bf16[128,4,128,128]{3,2,1,0:T(8,128)(2,1)} async-done(((bf16[2,4,128,128]{3,2,1,0:T(8,128)(2,1)}), bf16[128,4,128,128]{3,2,1,0:T(8,128)(2,1)}) %all-gather.13.cloned.1.call-update) | async-done | bytes 16777232 | tf_op jit(solution)/shard_map/all_gather | solution.py:18
  439.1 68.1 %while.34 = (s32[]{:T(128)}, f32[2,4,128,128]{3,2,1,0:T(8,128)S(1)}, s32[]{:T(128)}, bf16[64,2,4,128,128]{4,3,2,1,0:T(8,128)(2,1)}, s32[]{:T(128)}, /*index=5*/s32[]{:T(128)}, s32[]{:T(128)}, s32[]{:T(128)}) while((s32[]{:T(128)}, f32[2,4,128,128]{3,2,1,0:T(8,128)S(1)}, s32[]{:T(128)}, bf16[64,2,4,128,128]{4,3,2,1,0:T(8,128)(2,1)}, ...), condition=%wide.region_13.14_spmd, body=%wide.region_12.13_spmd.sunk | while | flops 262150 | bytes 1310855 | solution.py:25
  439.1 1.1 convert_add_fusion.8
  440.2 1.1 convert_add_fusion.8
  441.3 1.1 convert_add_fusion.8
  442.4 1.1 convert_add_fusion.8
  443.5 1.1 convert_add_fusion.8
  447.9 1.1 convert_add_fusion.8
  449.0 1.1 convert_add_fusion.8
  450.1 1.1 convert_add_fusion.8
  451.2 1.1 convert_add_fusion.8
  452.3 1.1 convert_add_fusion.8
  453.4 1.1 convert_add_fusion.8
  454.5 1.1 convert_add_fusion.8
  458.9 1.1 convert_add_fusion.8
  460.0 1.1 convert_add_fusion.8
  461.1 1.1 convert_add_fusion.8
  462.2 1.1 convert_add_fusion.8
  463.3 1.1 convert_add_fusion.8
  464.4 1.1 convert_add_fusion.8
  468.7 1.1 convert_add_fusion.8
  469.8 1.1 convert_add_fusion.8
  470.9 1.1 convert_add_fusion.8
  472.0 1.1 convert_add_fusion.8
  473.1 1.1 convert_add_fusion.8
  474.2 1.1 convert_add_fusion.8
  475.3 1.1 convert_add_fusion.8
  (110 shorter events, 54.5 us)
Async XLA Ops:
  7.2 3.3 copy-start.16
  7.2 3.4 copy-start.13
  7.2 108.1 %all-gather.9.cloned.1.call-start = ((), (), s32[]{:S(2)}) async-start(), calls=%async_computation | async-start | bytes 17039360 | tf_op jit(solution)/shard_map/all_gather | solution.py:18
  8.3 4.2 copy-start.12
  10.4 205.0 %all-gather.11.cloned.1.call-start = ((), (), s32[]{:S(2)}) async-start(), calls=%async_computation.1 | async-start | bytes 17039360 | tf_op jit(solution)/shard_map/all_gather | solution.py:18
  11.7 427.3 %all-gather.13.cloned.1.call-start = ((), (), s32[]{:S(2)}) async-start(), calls=%async_computation.2 | async-start | bytes 17039360 | tf_op jit(solution)/shard_map/all_gather | solution.py:18
  13.3 103.2 %copy-start.1 = (bf16[2,128,4,4,128]{4,3,2,1,0:T(4,128)(2,1)}, bf16[2,128,4,4,128]{4,3,2,1,0:T(4,128)(2,1)S(1)}, u32[]{:S(2)}) copy-start(bf16[2,128,4,4,128]{4,3,2,1,0:T(4,128)(2,1)S(1)} %reshape.126) | copy-start | bytes 3145732
  13.5 5.1 copy-start.14
  15.5 201.0 %copy-start.4 = (bf16[2,128,4,4,128]{4,3,2,1,0:T(4,128)(2,1)}, bf16[2,128,4,4,128]{4,3,2,1,0:T(4,128)(2,1)S(1)}, u32[]{:S(2)}) copy-start(bf16[2,128,4,4,128]{4,3,2,1,0:T(4,128)(2,1)S(1)} %reshape.129) | copy-start | bytes 3145732
  216.6 1.8 copy-start.7
  216.6 2.6 copy-start.10
  223.8 2.8 copy-start.17
  338.1 2.3 copy-start
  340.4 1.6 copy-start.2
  341.0 1.0 copy-start.5
  342.4 11.8 %copy-start.15 = (bf16[2,128,4,128,1]{1,3,4,2,0:T(8,128)(2,1)S(1)}, bf16[2,128,4,128,1]{1,3,4,2,0:T(8,128)(2,1)}, u32[]{:S(2)}) copy-start(bf16[2,128,4,128,1]{1,3,4,2,0:T(8,128)(2,1)} %copy-done.14) | copy-start | bytes 786436
  354.2 3.1 copy-start.8
  354.3 1.6 copy-start.6
  357.3 5.6 %copy-start.3 = (bf16[2,128,4,4,128]{4,3,2,1,0:T(4,128)(2,1)S(1)}, bf16[2,128,4,4,128]{4,3,2,1,0:T(4,128)(2,1)}, u32[]{:S(2)}) copy-start(bf16[2,128,4,4,128]{4,3,2,1,0:T(4,128)(2,1)} %copy-done.1) | copy-start | bytes 3145732
  360.3 2.6 copy-start.9
  439.0 68.1 %copy-start.11 = (f32[2,4,128,128]{3,2,1,0:T(8,128)S(1)}, f32[2,4,128,128]{3,2,1,0:T(8,128)}, u32[]{:S(2)}) copy-start(f32[2,4,128,128]{3,2,1,0:T(8,128)} %convolution_bitcast_fusion.1) | copy-start | bytes 1572868
Sparse Core Ops, SparseCore 0:
  11.4 103.9 all-gather.8
  118.7 96.7 all-gather.10
  343.4 95.5 all-gather.12
